TPU v7x, 512 devices: a whole 4x4x16 slice. The times are simulated.
512 devices in a mesh: grp: 16 (over y, x), dev: 32 (over z, core).
Axes of the slice: x: 4, y: 4, z: 16, core: 2. Of those that a mesh axis runs over, the one named last changes fastest.
Arguments:
- points: float32 [3, 524288], P(None, ('grp', 'dev')), may hold values from 0 to 2
- charges: float32 [16, 524288], P(None, ('grp', 'dev')), may hold values from -6 to 6
- morton: int32 [524288], P(('grp', 'dev')), may hold values from 0 to 1023, as said below
- neighbours: int32 [2048, 8], P(('grp', 'dev')), may hold values from 0 to 2047, as said below
- counts: int32 [2048], P(('grp', 'dev')), may hold values from 1 to 8
- skel_leaf: float32 [3, 524288], P(None, ('grp', 'dev')), may hold values from 0 to 2
- skel_block: float32 [3, 131072], P(None, ('grp', 'dev')), may hold values from 0 to 2
- skel_group: float32 [3, 4096], replicated, may hold values from 0 to 2
Outputs:
- potential: float32 [16, 524288], P(None, ('grp', 'dev'))
Inputs may be any that keep to these rules, and one draw needn't show every extreme that they name: `morton`: each aligned run of 1024 entries is a permutation of 0 to 1023. `neighbours`: entry [q, k] is a leaf other than q, at most 4 leaves away from q; only slots k < counts[q] are used.
All inputs are finite; a program needn't handle non-finite values.
Results may differ from a plain program's by a relative error of at most 0.0003.
Values sent between devices are 32-bit elements; how exact they have to be, the bound alone decides.
No kernel may reach another device: no remote copies, remote signals or barrier semaphores. Data moves between devices by JAX's collectives and lax.ppermute only.
A program may use at most 64 MiB of HBM per device.

v0:
```python
import math
import jax
import jax.numpy as jnp
from jax import lax
from jax.sharding import PartitionSpec as P

width_sq = 0.1
gain_factor = 5.0


def extended_2(cells, sides, width):
    for axis, dim in sides:
        count = lax.axis_size(axis)
        ends = count - 1
        head = lax.slice_in_dim(cells, 0, width, axis=dim)
        tail = lax.slice_in_dim(cells, cells.shape[dim] - width, cells.shape[dim], axis=dim)
        cells = jnp.concatenate(
            [
                lax.ppermute(tail, axis, [(i, (i + 1) % count) for i in range(ends)]),
                cells,
                lax.ppermute(head, axis, [((i + 1) % count, i) for i in range(ends)]),
            ],
            axis=dim,
        )
    return cells


def kernel_tile(source, target):
    distance = (source[0][:, None] - target[0][None, :]) ** 2
    distance = distance + (source[1][:, None] - target[1][None, :]) ** 2
    distance = distance + (source[2][:, None] - target[2][None, :]) ** 2
    return jnp.exp(-distance / width_sq)


def translate(values, source, target, term_count):
    product = jnp.dot(
        values,
        kernel_tile(source, target),
        precision=lax.Precision.HIGHEST,
        preferred_element_type=jnp.float32,
    )
    return gain_factor / math.sqrt(term_count) * product


def far_sum(running, weights, skeleton, target, own_member, skel_rank, term_count):
    span_cols = weights.shape[1]
    block_cols = min(skel_rank, span_cols)

    def one_block(block_index, partial_value):
        column = block_index * block_cols
        piece_w = lax.dynamic_slice_in_dim(weights, column, block_cols, 1)
        piece_s = lax.dynamic_slice_in_dim(skeleton, column, block_cols, 1)
        member = column // skel_rank
        keep_mask = jnp.where(member == own_member, 0.0, 1.0)
        return partial_value + keep_mask * translate(piece_w, piece_s, target, term_count)

    return lax.fori_loop(0, span_cols // block_cols, one_block, running)


def body(points, charges, morton, neighbours, counts, skel_leaf, skel_block, skel_group):
    n_groups = lax.axis_size("grp")
    n_blocks = lax.axis_size("dev")
    vectors, block_pts = charges.shape
    leaf_count = counts.shape[0]
    leaf_size = block_pts // leaf_count
    skel_rank = skel_block.shape[1]
    slot_total = neighbours.shape[1]
    group_id = lax.axis_index("grp")
    member_id = lax.axis_index("dev")
    block_id = group_id * n_blocks + member_id
    sorted_pts = jnp.take(points, morton, axis=1)
    sorted_chg = jnp.take(charges, morton, axis=1)
    leaf_pts = sorted_pts.reshape(3, leaf_count, leaf_size).transpose(1, 0, 2)
    leaf_chg = sorted_chg.reshape(vectors, leaf_count, leaf_size).transpose(1, 0, 2)
    leaf_skel = skel_leaf.reshape(3, leaf_count, skel_rank).transpose(1, 0, 2)
    leaf_weights = lax.map(
        lambda inputs: translate(inputs[0], inputs[1], inputs[2], leaf_size),
        (leaf_chg, leaf_pts, leaf_skel),
    )
    lifted = lax.map(
        lambda inputs: translate(inputs[0], inputs[1], skel_block, leaf_count * skel_rank),
        (leaf_weights, leaf_skel),
    )
    block_weights = jnp.sum(lifted, axis=0)
    own_group = lax.dynamic_slice_in_dim(skel_group, group_id * skel_rank, skel_rank, 1)
    raised = translate(block_weights, skel_block, own_group, n_blocks * skel_rank)
    empty = jnp.zeros((vectors, skel_rank), jnp.float32)
    group_terms = (n_groups - 1) * skel_rank
    group_weights = lax.psum(raised, "dev")
    group_field = far_sum(
        empty,
        lax.all_gather(group_weights, "grp", axis=1, tiled=True),
        skel_group,
        own_group,
        group_id,
        skel_rank,
        group_terms,
    )
    peer_field = far_sum(
        empty,
        lax.all_gather(block_weights, "dev", axis=1, tiled=True),
        lax.all_gather(skel_block, "dev", axis=1, tiled=True),
        skel_block,
        member_id,
        skel_rank,
        (n_blocks - 1) * skel_rank,
    )
    block_field = peer_field + translate(group_field, own_group, skel_block, skel_rank)
    leaf_field = lax.map(
        lambda target: translate(block_field, skel_block, target, skel_rank), leaf_skel
    )
    stacked = jnp.concatenate([sorted_pts, sorted_chg], axis=0)
    extended = extended_2(stacked, ((("grp", "dev"), 1),), block_pts)
    ext_leaves = extended.reshape(3 + vectors, 3 * leaf_count, leaf_size).transpose(1, 0, 2)
    first_leaf = block_id * leaf_count - leaf_count

    def near_leaf(inputs):
        own_pts, own_chg, own_field, own_skel, row_nbr, row_count = inputs
        direct = translate(own_chg, own_pts, own_pts, leaf_size)
        direct = direct + translate(own_field, own_skel, own_pts, skel_rank)

        def one_slot(slot_index, running):
            source = lax.dynamic_index_in_dim(
                ext_leaves, row_nbr[slot_index] - first_leaf, 0, keepdims=False
            )
            tile_term = translate(source[3:], source[:3], own_pts, leaf_size)
            return running + jnp.where(slot_index < row_count, tile_term, jnp.zeros_like(tile_term))

        return lax.fori_loop(0, slot_total, one_slot, direct)

    potential = lax.map(near_leaf, (leaf_pts, leaf_chg, leaf_field, leaf_skel, neighbours, counts))
    return potential.transpose(1, 0, 2).reshape(vectors, block_pts)


def solution(mesh):
    return jax.shard_map(
        body,
        mesh=mesh,
        in_specs=(
            P(None, ("grp", "dev")),
            P(None, ("grp", "dev")),
            P(("grp", "dev")),
            P(("grp", "dev"), None),
            P(("grp", "dev")),
            P(None, ("grp", "dev")),
            P(None, ("grp", "dev")),
            P(),
        ),
        out_specs=P(None, ("grp", "dev")),
        check_vma=False,
    )
```

profile of v0, /device:TPU:8, one launch (start us, length us, event | category | flops | bytes accessed | tf_op | source)
XLA Modules:
  0.0 328.9 jit_solution(2411669421259678028)
XLA Ops:
  0.8 0.9 copy.25
  1.7 2.8 gather_fusion.1
  5.8 2.8 gather_fusion
  9.0 12.9 %collective-permute-start.1 = (f32[19,1024]{1,0:T(8,128)S(1)}, f32[19,1024]{1,0:T(8,128)S(1)}, u32[]{:S(2)}, u32[]{:S(2)}) collective-permute-start(f32[19,1024]{1,0:T(8,128)S(1)} %pad_maximum_fusion.1), channel_id=1, source_target_pairs={{1,0},{2,1},{3,2},{4,3},{5,4},{6,5},{7,6},{8,7},{9,8},{10,9},{11,1... | collective-permute-start | bytes 233480 | tf_op jit(solution)/shard_map/ppermute | solution.py:21
  21.9 1.9 collective-permute-start
  24.6 27.1 %all_gather.10 = f32[3,8192]{1,0:T(4,128)S(1)} all-gather(f32[3,256]{1,0:T(4,128)S(1)} %copy-done), channel_id=1, replica_groups=mesh['grp'=16,'dev'=32] {'dev'}, dimensions={1}, use_global_device_ids=true | all-gather | bytes 101376 | tf_op jit(solution)/shard_map/all_gather | solution.py:102
  52.8 1.6 while.85
  54.5 1.7 while.86
  56.2 30.2 %all_gather.9 = f32[16,8192]{1,0:T(8,128)S(1)} all-gather(f32[16,256]{1,0:T(8,128)S(1)} %reduce_sum.9), channel_id=1, replica_groups=mesh['grp'=16,'dev'=32] {'dev'}, dimensions={1}, use_global_device_ids=true | all-gather | bytes 540672 | tf_op jit(solution)/shard_map/all_gather | solution.py:101
  88.3 90.3 %psum.7 = f32[16,256]{1,0:T(8,128)S(1)} all-reduce(f32[16,256]{1,0:T(8,128)S(1)} %convolution_multiply_fusion.7), channel_id=1, replica_groups=mesh['grp'=16,'dev'=32] {'dev'}, use_global_device_ids=true, to_apply=%region_7.8 | all-reduce | flops 4096 | bytes 32768 | tf_op jit(solution)/shard_map/psum | solution.py:89
  178.7 24.5 %all_gather.11 = f32[16,4096]{1,0:T(8,128)S(1)} all-gather(f32[16,256]{1,0:T(8,128)S(1)} %psum.7), channel_id=1, replica_groups=mesh['grp'=16,'dev'=32] {'grp'}, dimensions={1}, use_global_device_ids=true | all-gather | bytes 278528 | tf_op jit(solution)/shard_map/all_gather | solution.py:92
  203.1 21.3 %while.91 = (s32[]{:T(128)}, f32[16,256]{1,0:T(8,128)S(1)}, f32[16,4096]{1,0:T(8,128)S(1)}, f32[3,4096]{1,0:T(4,128)}, f32[3,256]{1,0:T(4,128)S(1)}, /*index=5*/...) while((s32[]{:T(128)}, f32[16,256]{1,0:T(8,128)S(1)}, ...), condition=%wide.region_9.10_spmd.clone, body=%wide.region_8.9_spmd.clone.sunk | while | flops 13250586 | bytes 68032 | solution.py:57
  203.1 0.9 constant_dynamic-slice_fusion.38
  204.5 0.9 constant_dynamic-slice_fusion.38
  207.1 0.9 constant_dynamic-slice_fusion.38
  209.8 0.9 constant_dynamic-slice_fusion.38
  211.1 0.9 constant_dynamic-slice_fusion.38
  224.4 17.1 %while.90 = (s32[]{:T(128)}, f32[16,256]{1,0:T(8,128)S(1)}, f32[16,8192]{1,0:T(8,128)S(1)}, f32[3,8192]{1,0:T(4,128)S(1)}, f32[3,256]{1,0:T(4,128)S(1)}, /*index...) while((s32[]{:T(128)}, f32[16,256]{1,0:T(8,128)S(1)}, ...), condition=%wide.region_6.7_spmd.clone, body=%wide.region_5.6_spmd.clone.sunk | while | flops 13250586 | bytes 68032 | solution.py:57
  241.9 1.8 while.87
  244.7 83.6 %while.89 = (s32[]{:T(128)}, f32[4,16,256]{2,1,0:T(8,128)S(1)}, f32[4,16,256]{2,1,0:T(8,128)S(1)}, f32[4,3,256]{2,1,0:T(4,128)S(1)}, f32[4,16,256]{2,1,0:T(8,128...) while((s32[]{:T(128)}, f32[4,16,256]{2,1,0:T(8,128)S(1)}, ...), condition=%wide.region_15.16_spmd, body=%wide.region_12.15_spmd.sunk | while | flops 39735312 | bytes 213682 | solution.py:131
  246.8 18.8 %while.92 = (s32[]{:T(128)}, f32[16,256]{1,0:T(8,128)S(1)}, s32[]{:T(128)}, s32[8]{0:T(128)S(1)}, s32[]{:T(128)}, /*index=5*/f32[12,19,256]{2,1,0:T(8,128)S(1)},...) while((s32[]{:T(128)}, f32[16,256]{1,0:T(8,128)S(1)}, ...), condition=%wide.region_14.14_spmd, body=%wide.region_13.13_spmd.sunk | while | flops 13250570 | bytes 67841 | solution.py:129
  267.6 18.8 %while.92 = (s32[]{:T(128)}, f32[16,256]{1,0:T(8,128)S(1)}, s32[]{:T(128)}, s32[8]{0:T(128)S(1)}, s32[]{:T(128)}, /*index=5*/f32[12,19,256]{2,1,0:T(8,128)S(1)},...) while((s32[]{:T(128)}, f32[16,256]{1,0:T(8,128)S(1)}, ...), condition=%wide.region_14.14_spmd, body=%wide.region_13.13_spmd.sunk | while | flops 13250570 | bytes 67841 | solution.py:129
  288.5 18.8 %while.92 = (s32[]{:T(128)}, f32[16,256]{1,0:T(8,128)S(1)}, s32[]{:T(128)}, s32[8]{0:T(128)S(1)}, s32[]{:T(128)}, /*index=5*/f32[12,19,256]{2,1,0:T(8,128)S(1)},...) while((s32[]{:T(128)}, f32[16,256]{1,0:T(8,128)S(1)}, ...), condition=%wide.region_14.14_spmd, body=%wide.region_13.13_spmd.sunk | while | flops 13250570 | bytes 67841 | solution.py:129
  309.4 18.8 %while.92 = (s32[]{:T(128)}, f32[16,256]{1,0:T(8,128)S(1)}, s32[]{:T(128)}, s32[8]{0:T(128)S(1)}, s32[]{:T(128)}, /*index=5*/f32[12,19,256]{2,1,0:T(8,128)S(1)},...) while((s32[]{:T(128)}, f32[16,256]{1,0:T(8,128)S(1)}, ...), condition=%wide.region_14.14_spmd, body=%wide.region_13.13_spmd.sunk | while | flops 13250570 | bytes 67841 | solution.py:129
  (320 shorter events, 85.6 us)
Async XLA Ops:
  0.0 0.8 copy-start.3
  4.7 0.8 copy-start.2
  9.0 234.7 %collective-permute-start.1 = (f32[19,1024]{1,0:T(8,128)S(1)}, f32[19,1024]{1,0:T(8,128)S(1)}, u32[]{:S(2)}, u32[]{:S(2)}) collective-permute-start(f32[19,1024]{1,0:T(8,128)S(1)} %pad_maximum_fusion.1), channel_id=1, source_target_pairs={{1,0},{2,1},{3,2},{4,3},{5,4},{6,5},{7,6},{8,7},{9,8},{10,9},{11,1... | collective-permute-start | bytes 233480 | tf_op jit(solution)/shard_map/ppermute | solution.py:21
  21.9 221.8 %collective-permute-start = (f32[19,1024]{1,0:T(8,128)S(1)}, f32[19,1024]{1,0:T(8,128)S(1)}, u32[]{:S(2)}, u32[]{:S(2)}) collective-permute-start(f32[19,1024]{1,0:T(8,128)S(1)} %pad_maximum_fusion.1), channel_id=1, source_target_pairs={{0,1},{1,2},{2,3},{3,4},{4,5},{5,6},{6,7},{7,8},{8,9},{9,10},{10,1... | collective-permute-start | bytes 233480 | tf_op jit(solution)/shard_map/ppermute | solution.py:19
  23.9 0.7 copy-start
  52.1 0.7 copy-start.1
  244.0 0.7 copy-start.4
where the time goes:
time: 331 us; the launch traced here: 329 us
  blocking collectives  172 us (52%)
  local copies, waits for them, and re-layouts  55.4 us (17%)
  loops' own time  45.1 us (14%)
  matrix products  39.9 us (12%)
  starting transfers between devices  14.8 us (4%)
    psum x1, blocking collectives, body(): group_weights = lax.psum(raised, 'dev')  90.3 us
    another operation x4, loops' own time, near_leaf(): return lax.fori_loop(0, slot_total, one_slot, direct)  41.7 us
    dot_general x102, matrix products, translate(): jnp.dot(values, kernel_tile(source, target), precision=lax.Precision.HIGH...  39.9 us
    all_gather x1, blocking collectives, body(): lax.all_gather(block_weights, 'dev', axis=1, tiled=True)  30.2 us
    all_gather x1, blocking collectives, body(): lax.all_gather(skel_block, 'dev', axis=1, tiled=True)  27.1 us
    all_gather x1, blocking collectives, body(): lax.all_gather(group_weights, 'grp', axis=1, tiled=True)  24.5 us
    dynamic_slice x32, local copies, waits for them, and re-layouts, one_slot(): row_nbr[slot_index] - first_leaf  19.9 us
    slice x138, local copies, waits for them, and re-layouts, kernel_tile(): distance = (source[0][:, None] - target[0][None, :]) ** 2  18.6 us
  transfers between devices with their start and end apart: 2, of which 0 were waited for; matrix products, arithmetic and copies ran while one was open for 13% of the time, Pallas kernels for 0%

commit v1 on v0

--- a/solution.py
+++ b/solution.py
@@ -86,7 +86,13 @@
     raised = translate(block_weights, skel_block, own_group, n_blocks * skel_rank)
     empty = jnp.zeros((vectors, skel_rank), jnp.float32)
     group_terms = (n_groups - 1) * skel_rank
-    group_weights = lax.psum(raised, "dev")
+    group_weights = raised
+    n = lax.axis_size("dev")
+    for nth in [pp for pp in (1, 2, 4, 8, 16) if pp < n]:
+        runs = []
+        for at in range(n):
+            runs.append((at, at ^ nth))
+        group_weights = group_weights + lax.ppermute(group_weights, axis_name="dev", perm=runs)
     group_field = far_sum(
         empty,
         lax.all_gather(group_weights, "grp", axis=1, tiled=True),

time: 331 us -> 272 us (0.82)
  blocking collectives: 172 us -> 84.8 us
  starting transfers between devices: 14.8 us -> 31.5 us
  waiting for transfers between devices: 0.01 us -> 12.5 us
    psum x1 -> x0, blocking collectives: 90.3 us -> none  [body(): group_weights = lax.psum(raised, 'dev')]
    ppermute x0 -> x5, starting transfers between devices: none -> 16.6 us  [body(): lax.ppermute(group_weights, axis_name='dev', perm=runs)]
    ppermute x0 -> x5, waiting for transfers between devices: none -> 12.5 us  [body(): lax.ppermute(group_weights, axis_name='dev', perm=runs)]
  transfers between devices with their start and end apart: 2 -> 7, of which waited for: 0 -> 2; matrix products, arithmetic and copies ran while one was open for 13% -> 8% of each run, Pallas kernels for 0% -> 0%
where the time goes in v1:
time: 272 us; the launch traced here: 270 us
  blocking collectives  84.8 us (31%)
  local copies, waits for them, and re-layouts  55.5 us (20%)
  loops' own time  44.7 us (16%)
  matrix products  39.9 us (15%)
  starting transfers between devices  31.5 us (12%)
  waiting for transfers between devices  12.5 us (5%)
    another operation x4, loops' own time, near_leaf(): return lax.fori_loop(0, slot_total, one_slot, direct)  41.3 us
    dot_general x102, matrix products, translate(): jnp.dot(values, kernel_tile(source, target), precision=lax.Precision.HIGH...  39.9 us
    all_gather x1, blocking collectives, body(): lax.all_gather(block_weights, 'dev', axis=1, tiled=True)  30.3 us
    all_gather x1, blocking collectives, body(): lax.all_gather(skel_block, 'dev', axis=1, tiled=True)  29.1 us
    all_gather x1, blocking collectives, body(): lax.all_gather(group_weights, 'grp', axis=1, tiled=True)  25.4 us
    dynamic_slice x32, local copies, waits for them, and re-layouts, one_slot(): row_nbr[slot_index] - first_leaf  19.9 us
    slice x138, local copies, waits for them, and re-layouts, kernel_tile(): distance = (source[0][:, None] - target[0][None, :]) ** 2  18.6 us
    ppermute x5, starting transfers between devices, body(): lax.ppermute(group_weights, axis_name='dev', perm=runs)  16.6 us
  transfers between devices with their start and end apart: 7, of which 2 were waited for; matrix products, arithmetic and copies ran while one was open for 8% of the time, Pallas kernels for 0%

profile of v1, /device:TPU:8, one launch (start us, length us, event | category | flops | bytes accessed | tf_op | source)
XLA Modules:
  0.0 270.4 jit_solution(9075619175361322617)
XLA Ops:
  1.7 2.8 %gather_fusion.1 = f32[1024,3]{1,0:T(8,128)S(1)} fusion(f32[3,1024]{0,1:T(8,128)S(1)} %copy.25, s32[1024]{0:T(1024)S(1)} %fusion.219), kind=kCustom, calls=%fused_computation.1 | custom fusion | bytes 28672 | tf_op jit(solution)/shard_map/jit(_take)/gather | solution.py:71
  5.8 2.8 %gather_fusion = f32[1024,16]{1,0:T(8,128)S(1)} fusion(f32[16,1024]{0,1:T(8,128)S(1)} %copy.23, s32[1024]{0:T(1024)S(1)} %fusion.219), kind=kCustom, calls=%fused_computation | custom fusion | bytes 135168 | tf_op jit(solution)/shard_map/jit(_take)/gather | solution.py:72
  9.0 12.9 %collective-permute-start.6 = (f32[19,1024]{1,0:T(8,128)S(1)}, f32[19,1024]{1,0:T(8,128)S(1)}, u32[]{:S(2)}, u32[]{:S(2)}) collective-permute-start(f32[19,1024]{1,0:T(8,128)S(1)} %pad_maximum_fusion.1), channel_id=1, source_target_pairs={{1,0},{2,1},{3,2},{4,3},{5,4},{6,5},{7,6},{8,7},{9,8},{10,9},{11,1... | collective-permute-start | bytes 233480 | tf_op jit(solution)/shard_map/ppermute | solution.py:21
  21.9 1.9 collective-permute-start.5
  25.7 1.6 while.85
  27.4 1.7 while.86
  30.4 1.9 collective-permute-start
  32.3 30.3 %all_gather.9 = f32[16,8192]{1,0:T(8,128)S(1)} all-gather(f32[16,256]{1,0:T(8,128)S(1)} %reduce_sum.9), channel_id=1, replica_groups=mesh['grp'=16,'dev'=32] {'dev'}, dimensions={1}, use_global_device_ids=true | all-gather | bytes 540672 | tf_op jit(solution)/shard_map/all_gather | solution.py:107
  62.7 1.9 collective-permute-start.1
  64.6 29.1 %all_gather.10 = f32[3,8192]{1,0:T(4,128)S(1)} all-gather(f32[3,256]{1,0:T(4,128)S(1)} %get-tuple-element.1438), channel_id=1, replica_groups=mesh['grp'=16,'dev'=32] {'dev'}, dimensions={1}, use_global_device_ids=true | all-gather | bytes 101376 | tf_op jit(solution)/shard_map/all_gather | solution.py:108
  93.7 2.2 collective-permute-start.2
  95.9 17.1 %while.90 = (s32[]{:T(128)}, f32[16,256]{1,0:T(8,128)S(1)}, f32[16,8192]{1,0:T(8,128)S(1)}, f32[3,8192]{1,0:T(4,128)S(1)}, f32[3,256]{1,0:T(4,128)S(1)}, /*index...) while((s32[]{:T(128)}, f32[16,256]{1,0:T(8,128)S(1)}, ...), condition=%wide.region_6.7_spmd.clone, body=%wide.region_5.6_spmd.clone.sunk | while | flops 13250586 | bytes 68032 | solution.py:57
  113.0 4.3 %collective-permute-start.3 = (f32[16,256]{1,0:T(8,128)S(1)}, f32[16,256]{1,0:T(8,128)S(1)}, u32[]{:S(2)}, u32[]{:S(2)}) collective-permute-start(f32[16,256]{1,0:T(8,128)S(1)} %add.285), channel_id=1, source_target_pairs={{0,8},{1,9},{2,10},{3,11},{4,12},{5,13},{6,14},{7,15},{8,0},{9,1},... | collective-permute-start | bytes 49160 | tf_op jit(solution)/shard_map/ppermute | solution.py:95
  118.0 4.6 %collective-permute-done.3 = f32[16,256]{1,0:T(8,128)S(1)} collective-permute-done((f32[16,256]{1,0:T(8,128)S(1)}, f32[16,256]{1,0:T(8,128)S(1)}, u32[]{:S(2)}, u32[]{:S(2)}) %collective-permute-start.3) | collective-permute-done | bytes 16416 | tf_op jit(solution)/shard_map/ppermute | solution.py:95
  122.6 6.3 %collective-permute-start.4 = (f32[16,256]{1,0:T(8,128)S(1)}, f32[16,256]{1,0:T(8,128)S(1)}, u32[]{:S(2)}, u32[]{:S(2)}) collective-permute-start(f32[16,256]{1,0:T(8,128)S(1)} %add.286), channel_id=1, source_target_pairs={{0,16},{1,17},{2,18},{3,19},{4,20},{5,21},{6,22},{7,23},{8,24},{9,... | collective-permute-start | bytes 49160 | tf_op jit(solution)/shard_map/ppermute | solution.py:95
  129.2 7.9 %collective-permute-done.4 = f32[16,256]{1,0:T(8,128)S(1)} collective-permute-done((f32[16,256]{1,0:T(8,128)S(1)}, f32[16,256]{1,0:T(8,128)S(1)}, u32[]{:S(2)}, u32[]{:S(2)}) %collective-permute-start.4) | collective-permute-done | bytes 16416 | tf_op jit(solution)/shard_map/ppermute | solution.py:95
  137.1 25.4 %all_gather.11 = f32[16,4096]{1,0:T(8,128)S(1)} all-gather(f32[16,256]{1,0:T(8,128)S(1)} %add.287), channel_id=1, replica_groups=mesh['grp'=16,'dev'=32] {'grp'}, dimensions={1}, use_global_device_ids=true | all-gather | bytes 278528 | tf_op jit(solution)/shard_map/all_gather | solution.py:98
  162.4 21.3 %while.91 = (s32[]{:T(128)}, f32[16,256]{1,0:T(8,128)S(1)}, f32[16,4096]{1,0:T(8,128)S(1)}, f32[3,4096]{1,0:T(4,128)}, f32[3,256]{1,0:T(4,128)S(1)}, /*index=5*/...) while((s32[]{:T(128)}, f32[16,256]{1,0:T(8,128)S(1)}, ...), condition=%wide.region_8.9_spmd.clone, body=%wide.region_7.8_spmd.clone.sunk | while | flops 13250586 | bytes 68032 | solution.py:57
  184.1 1.8 while.87
  186.6 83.2 %while.89 = (s32[]{:T(128)}, f32[4,16,256]{2,1,0:T(8,128)S(1)}, f32[4,16,256]{2,1,0:T(8,128)S(1)}, f32[4,3,256]{2,1,0:T(4,128)S(1)}, f32[4,16,256]{2,1,0:T(8,128...) while((s32[]{:T(128)}, f32[4,16,256]{2,1,0:T(8,128)S(1)}, ...), condition=%wide.region_14.15_spmd, body=%wide.region_11.14_spmd.sunk | while | flops 39735312 | bytes 213682 | solution.py:137
  188.7 18.7 %while.92 = (s32[]{:T(128)}, f32[16,256]{1,0:T(8,128)S(1)}, s32[]{:T(128)}, s32[8]{0:T(128)S(1)}, s32[]{:T(128)}, /*index=5*/f32[12,19,256]{2,1,0:T(8,128)S(1)},...) while((s32[]{:T(128)}, f32[16,256]{1,0:T(8,128)S(1)}, ...), condition=%wide.region_13.13_spmd, body=%wide.region_12.12_spmd.sunk | while | flops 13250570 | bytes 67841 | solution.py:135
  209.5 18.7 %while.92 = (s32[]{:T(128)}, f32[16,256]{1,0:T(8,128)S(1)}, s32[]{:T(128)}, s32[8]{0:T(128)S(1)}, s32[]{:T(128)}, /*index=5*/f32[12,19,256]{2,1,0:T(8,128)S(1)},...) while((s32[]{:T(128)}, f32[16,256]{1,0:T(8,128)S(1)}, ...), condition=%wide.region_13.13_spmd, body=%wide.region_12.12_spmd.sunk | while | flops 13250570 | bytes 67841 | solution.py:135
  230.3 18.7 %while.92 = (s32[]{:T(128)}, f32[16,256]{1,0:T(8,128)S(1)}, s32[]{:T(128)}, s32[8]{0:T(128)S(1)}, s32[]{:T(128)}, /*index=5*/f32[12,19,256]{2,1,0:T(8,128)S(1)},...) while((s32[]{:T(128)}, f32[16,256]{1,0:T(8,128)S(1)}, ...), condition=%wide.region_13.13_spmd, body=%wide.region_12.12_spmd.sunk | while | flops 13250570 | bytes 67841 | solution.py:135
  251.1 18.7 %while.92 = (s32[]{:T(128)}, f32[16,256]{1,0:T(8,128)S(1)}, s32[]{:T(128)}, s32[8]{0:T(128)S(1)}, s32[]{:T(128)}, /*index=5*/f32[12,19,256]{2,1,0:T(8,128)S(1)},...) while((s32[]{:T(128)}, f32[16,256]{1,0:T(8,128)S(1)}, ...), condition=%wide.region_13.13_spmd, body=%wide.region_12.12_spmd.sunk | while | flops 13250570 | bytes 67841 | solution.py:135
  (334 shorter events, 91.0 us)
Async XLA Ops:
  0.0 0.8 copy-start.3
  4.7 0.8 copy-start.2
  9.0 119.9 %collective-permute-start.6 = (f32[19,1024]{1,0:T(8,128)S(1)}, f32[19,1024]{1,0:T(8,128)S(1)}, u32[]{:S(2)}, u32[]{:S(2)}) collective-permute-start(f32[19,1024]{1,0:T(8,128)S(1)} %pad_maximum_fusion.1), channel_id=1, source_target_pairs={{1,0},{2,1},{3,2},{4,3},{5,4},{6,5},{7,6},{8,7},{9,8},{10,9},{11,1... | collective-permute-start | bytes 233480 | tf_op jit(solution)/shard_map/ppermute | solution.py:21
  21.9 107.0 %collective-permute-start.5 = (f32[19,1024]{1,0:T(8,128)S(1)}, f32[19,1024]{1,0:T(8,128)S(1)}, u32[]{:S(2)}, u32[]{:S(2)}) collective-permute-start(f32[19,1024]{1,0:T(8,128)S(1)} %pad_maximum_fusion.1), channel_id=1, source_target_pairs={{0,1},{1,2},{2,3},{3,4},{4,5},{5,6},{6,7},{7,8},{8,9},{9,10},{10,1... | collective-permute-start | bytes 233480 | tf_op jit(solution)/shard_map/ppermute | solution.py:19
  23.9 0.7 copy-start
  25.0 0.7 copy-start.1
  30.4 32.3 %collective-permute-start = (f32[16,256]{1,0:T(8,128)S(1)}, f32[16,256]{1,0:T(8,128)S(1)}, u32[]{:S(2)}, u32[]{:S(2)}) collective-permute-start(f32[16,256]{1,0:T(8,128)S(1)} %convolution_multiply_fusion.7), channel_id=1, source_target_pairs={{0,1},{1,0},{2,3},{3,2},{4,5},{5,4},{6,7},{7,6},{8,9},{9,8},{10,11... | collective-permute-start | bytes 49160 | tf_op jit(solution)/shard_map/ppermute | solution.py:95
  62.7 31.1 %collective-permute-start.1 = (f32[16,256]{1,0:T(8,128)S(1)}, f32[16,256]{1,0:T(8,128)S(1)}, u32[]{:S(2)}, u32[]{:S(2)}) collective-permute-start(f32[16,256]{1,0:T(8,128)S(1)} %add.283), channel_id=1, source_target_pairs={{0,2},{1,3},{2,0},{3,1},{4,6},{5,7},{6,4},{7,5},{8,10},{9,11},{10,... | collective-permute-start | bytes 49160 | tf_op jit(solution)/shard_map/ppermute | solution.py:95
  93.7 19.3 %collective-permute-start.2 = (f32[16,256]{1,0:T(8,128)S(1)}, f32[16,256]{1,0:T(8,128)S(1)}, u32[]{:S(2)}, u32[]{:S(2)}) collective-permute-start(f32[16,256]{1,0:T(8,128)S(1)} %add.284), channel_id=1, source_target_pairs={{0,4},{1,5},{2,6},{3,7},{4,0},{5,1},{6,2},{7,3},{8,12},{9,13},{10,... | collective-permute-start | bytes 49160 | tf_op jit(solution)/shard_map/ppermute | solution.py:95
  113.0 9.5 %collective-permute-start.3 = (f32[16,256]{1,0:T(8,128)S(1)}, f32[16,256]{1,0:T(8,128)S(1)}, u32[]{:S(2)}, u32[]{:S(2)}) collective-permute-start(f32[16,256]{1,0:T(8,128)S(1)} %add.285), channel_id=1, source_target_pairs={{0,8},{1,9},{2,10},{3,11},{4,12},{5,13},{6,14},{7,15},{8,0},{9,1},... | collective-permute-start | bytes 49160 | tf_op jit(solution)/shard_map/ppermute | solution.py:95
  122.6 14.5 %collective-permute-start.4 = (f32[16,256]{1,0:T(8,128)S(1)}, f32[16,256]{1,0:T(8,128)S(1)}, u32[]{:S(2)}, u32[]{:S(2)}) collective-permute-start(f32[16,256]{1,0:T(8,128)S(1)} %add.286), channel_id=1, source_target_pairs={{0,16},{1,17},{2,18},{3,19},{4,20},{5,21},{6,22},{7,23},{8,24},{9,... | collective-permute-start | bytes 49160 | tf_op jit(solution)/shard_map/ppermute | solution.py:95
  185.9 0.7 copy-start.4
